TPU v7x, 256 devices: a whole 4x4x8 slice. The times are simulated.
256 devices in a mesh: depth: 4 (over x), tile: 64 (over y, z, core).
Axes of the slice: x: 4, y: 4, z: 8, core: 2. Of those that a mesh axis runs over, the one named last changes fastest.
Arguments:
- source: bfloat16 [128, 2, 128, 256], P('tile'), may hold values from -6 to 6
- anchors: int32 [128], P('tile'), may hold values from -256 to 16128, as said below
- counts: int32 [4], P('depth'), may hold values from 1 to 3, 8 in all
- reflect: bfloat16 [4, 3, 128, 16384], P('depth', None, None, 'tile'), may hold values from -0.3984375 to 0.3984375
- lateral_x: bfloat16 [4, 3, 2, 128, 128], P('depth'), may hold values from -0.375 to 0.375
- lateral_y: bfloat16 [4, 3, 2, 256, 256], P('depth'), may hold values from -0.25 to 0.25
Outputs:
- image: float32 [4, 3, 128, 16384], P('depth', None, None, 'tile')
Inputs may be any that keep to these rules, and one draw needn't show every extreme that they name: `anchors`: the shots held by tile index t start their aperture between (t - 1) * 256 and t * 256. The counts sum to 8; slots at or past a section's count are unused.
All inputs are finite; a program needn't handle non-finite values. No bound on the sum of `counts` on one device may be relied on, other than what follows from the above.
Results may differ from a plain program's by a relative error of at most 0.023.
Values may be sent and summed in bfloat16 or wider, within the bound.
A program may use at most 64 MiB of HBM per device.

v0:
```python
import jax
import jax.numpy as jnp
from jax import lax
from jax.sharding import PartitionSpec as P


def padded(array, sides, width):
    for axis, dim in sides:
        size, length = (lax.axis_size(axis), array.shape[dim])
        up = [(i, (i + 1) % size) for i in range(size - 1)]
        down = [(j, i) for i, j in up]
        last = lax.slice_in_dim(array, length - width, length, axis=dim)
        leading = lax.slice_in_dim(array, 0, width, axis=dim)
        before = lax.ppermute(last, axis, up)
        after = lax.ppermute(leading, axis, down)
        array = jnp.concatenate([before, array, after], axis=dim)
    return array


def shifted(array, axis, by):
    length = lax.axis_size(axis)
    pairs = [(i, i + by) for i in range(length) if 0 <= i + by < length]
    return lax.ppermute(array, axis, pairs)


def pair_product(einsum_form, first_pair, second_pair):
    real_part = jnp.einsum(
        einsum_form, first_pair[0], second_pair[0], preferred_element_type=jnp.float32
    ) - jnp.einsum(einsum_form, first_pair[1], second_pair[1], preferred_element_type=jnp.float32)
    imag_part = jnp.einsum(
        einsum_form, first_pair[0], second_pair[1], preferred_element_type=jnp.float32
    ) + jnp.einsum(einsum_form, first_pair[1], second_pair[0], preferred_element_type=jnp.float32)
    return jnp.stack([real_part, imag_part], axis=1)


def descend_levels(entering, part_refl, op_first, op_second, active):
    wavefield = entering
    stored = []
    for level_slot in range(part_refl.shape[1]):
        stored.append(wavefield)

        def descend_advance(current, level_slot=level_slot):
            gain_factor = 1.0 + part_refl[:, level_slot].astype(jnp.float32)
            scaled = (gain_factor[:, None] * current.astype(jnp.float32)).astype(jnp.bfloat16)
            middle = pair_product(
                "ab,kby->kay",
                (op_first[level_slot, 0], op_first[level_slot, 1]),
                (scaled[:, 0], scaled[:, 1]),
            ).astype(jnp.bfloat16)
            moved = pair_product(
                "kxb,ab->kxa",
                (middle[:, 0], middle[:, 1]),
                (op_second[level_slot, 0], op_second[level_slot, 1]),
            )
            return moved.astype(jnp.bfloat16)

        wavefield = lax.cond(
            active[level_slot], descend_advance, lambda current: current, wavefield
        )
    return (jnp.stack(stored, axis=1), wavefield)


def ascend_levels(entering, stored, part_refl, op_first, op_second, active):
    upgoing = entering
    depth_slots = part_refl.shape[1]
    per_level = [None] * depth_slots
    for level_slot in reversed(range(depth_slots)):
        downgoing = stored[:, level_slot]

        def ascend_advance(current, downward, level_slot=level_slot):
            back_wave = pair_product(
                "ba,kby->kay",
                (op_first[level_slot, 0], op_first[level_slot, 1]),
                (current[:, 0], current[:, 1]),
            ).astype(jnp.bfloat16)
            spread = pair_product(
                "kxb,ba->kxa",
                (back_wave[:, 0], back_wave[:, 1]),
                (op_second[level_slot, 0], op_second[level_slot, 1]),
            )
            reflected = part_refl[:, level_slot].astype(jnp.float32)[:, None] * downward.astype(
                jnp.float32
            )
            return (reflected + spread).astype(jnp.bfloat16)

        def keep_wave(current, downward):
            return current

        upgoing = lax.cond(active[level_slot], ascend_advance, keep_wave, upgoing, downgoing)
        product_pair = downgoing.astype(jnp.float32) * upgoing.astype(jnp.float32)
        per_level[level_slot] = jnp.where(
            active[level_slot], product_pair[:, 0] + product_pair[:, 1], jnp.float32(0.0)
        )
    return (jnp.stack(per_level, axis=1), upgoing)


def place_shots(canvas, correlations, offsets):
    for shot_index in range(correlations.shape[0]):
        placed = (
            lax.dynamic_slice_in_dim(canvas, offsets[shot_index], correlations.shape[3], 2)
            + correlations[shot_index]
        )
        canvas = lax.dynamic_update_slice_in_dim(canvas, placed, offsets[shot_index], 2)
    return canvas


def on_device(source, anchors, counts, reflect, lateral_x, lateral_y):
    shot_count = source.shape[0]
    depth_slots = reflect.shape[1]
    rows_first = source.shape[2]
    aperture = source.shape[3]
    tile_width = reflect.shape[3]
    sections = lax.axis_size("depth")
    section = lax.axis_index("depth")
    tile_place = lax.axis_index("tile")
    widened = padded(reflect[0], (("tile", 2),), tile_width)
    offsets = anchors - (tile_place - 1) * tile_width
    level_count = counts[0]
    active = jnp.arange(depth_slots, dtype=jnp.int32) < level_count
    op_first = lateral_x[0]
    op_second = lateral_y[0]
    windows = jax.vmap(lambda offset: lax.dynamic_slice_in_dim(widened, offset, aperture, 2))(
        offsets
    )
    batches = 1
    batch_size = shot_count // batches
    steps_total = sections + batches - 1
    stored = jnp.zeros((shot_count, depth_slots, 2, rows_first, aperture), jnp.bfloat16)
    arriving = jnp.zeros((batch_size, 2, rows_first, aperture), jnp.bfloat16)
    for segment_step in range(steps_total):
        batch_index = segment_step - section
        is_active = (batch_index >= 0) & (batch_index < batches)
        first_row = jnp.clip(batch_index, 0, batches - 1) * batch_size
        entering = jnp.where(section == 0, source, arriving)
        part_refl = windows

        def descend_work(entering, part_refl, stored, first_row):
            levels, leaving = descend_levels(entering, part_refl, op_first, op_second, active)
            return (lax.dynamic_update_slice_in_dim(stored, levels, first_row, 0), leaving)

        def skip_work(entering, part_refl, stored, first_row):
            return (stored, entering)

        stored, leaving = lax.cond(
            is_active, descend_work, skip_work, entering, part_refl, stored, first_row
        )
        if segment_step + 1 < steps_total:
            arriving = shifted(leaving, "depth", 1)
    correlations = jnp.zeros((shot_count, depth_slots, rows_first, aperture), jnp.float32)
    arriving = jnp.zeros((batch_size, 2, rows_first, aperture), jnp.bfloat16)
    for segment_step in range(steps_total):
        batch_index = segment_step - (sections - 1 - section)
        is_active = (batch_index >= 0) & (batch_index < batches)
        first_row = jnp.clip(batch_index, 0, batches - 1) * batch_size
        entering = jnp.where(section == sections - 1, jnp.zeros_like(arriving), arriving)
        part_refl = windows
        part_down = stored

        def ascend_work(entering, part_refl, part_down, correlations, first_row):
            levels, leaving = ascend_levels(
                entering, part_down, part_refl, op_first, op_second, active
            )
            return (lax.dynamic_update_slice_in_dim(correlations, levels, first_row, 0), leaving)

        def spare_work(entering, part_refl, part_down, correlations, first_row):
            return (correlations, entering)

        correlations, leaving = lax.cond(
            is_active,
            ascend_work,
            spare_work,
            entering,
            part_refl,
            part_down,
            correlations,
            first_row,
        )
        if segment_step + 1 < steps_total:
            arriving = shifted(leaving, "depth", -1)
    canvas = jnp.zeros((depth_slots, rows_first, 3 * tile_width), jnp.float32)
    canvas = place_shots(canvas, correlations, offsets)
    with_rims = padded(canvas.astype(jnp.bfloat16), (("tile", 2),), tile_width).astype(canvas.dtype)
    image_tile = (
        with_rims[:, :, :tile_width]
        + with_rims[:, :, 2 * tile_width : 3 * tile_width]
        + with_rims[:, :, 4 * tile_width :]
    )
    return image_tile[None]


def solution(mesh):
    return jax.shard_map(
        on_device,
        mesh=mesh,
        in_specs=(
            P("tile", None, None, None),
            P("tile"),
            P("depth"),
            P("depth", None, None, "tile"),
            P("depth", None, None, None, None),
            P("depth", None, None, None, None),
        ),
        out_specs=P("depth", None, None, "tile"),
        check_vma=False,
    )
```

profile of v0, /device:TPU:1, one launch (start us, length us, event | category | flops | bytes accessed | tf_op | source)
XLA Modules:
  0.0 183.3 jit_solution(8696592301896181706)
XLA Ops:
  0.0 1.1 copy.123
  1.1 4.9 %collective-permute-start = (bf16[3,128,256]{1,0,2:T(4,128)(2,1)S(1)}, bf16[3,128,256]{1,0,2:T(4,128)(2,1)S(1)}, u32[]{:S(2)}, u32[]{:S(2)}) collective-permute-start(bf16[3,128,256]{1,0,2:T(4,128)(2,1)S(1)} %bitcast.1299), channel_id=1, source_target_pairs={{0,1},{1,2},{2,3},{3,4},{4,5},{5,6},{6,7},{7,8},{8,9},{9,10},{10,1... | collective-permute-start | bytes 589832 | tf_op jit(solution)/shard_map/ppermute | solution.py:14
  6.1 1.9 %collective-permute-start.1 = (bf16[3,128,256]{1,0,2:T(4,128)(2,1)S(1)}, bf16[3,128,256]{1,0,2:T(4,128)(2,1)S(1)}, u32[]{:S(2)}, u32[]{:S(2)}) collective-permute-start(bf16[3,128,256]{1,0,2:T(4,128)(2,1)S(1)} %bitcast.1300), channel_id=1, source_target_pairs={{1,0},{2,1},{3,2},{4,3},{5,4},{6,5},{7,6},{8,7},{9,8},{10,9},{11,1... | collective-permute-start | bytes 589832 | tf_op jit(solution)/shard_map/ppermute | solution.py:15
  8.0 1.1 copy.133
  9.9 3.9 %collective-permute-done.1 = bf16[3,128,256]{1,0,2:T(4,128)(2,1)S(1)} collective-permute-done((bf16[3,128,256]{1,0,2:T(4,128)(2,1)S(1)}, bf16[3,128,256]{1,0,2:T(4,128)(2,1)S(1)}, u32[]{:S(2)}, u32[]{:S(2)}) %collective-permute-start.1) | collective-permute-done | bytes 196640 | tf_op jit(solution)/shard_map/ppermute | solution.py:15
  13.8 0.5 pad_maximum_fusion.19
  14.3 1.0 gather_fusion
  15.4 12.9 %conditional.31 = (bf16[2,3,2,128,256]{4,3,0,2,1:T(8,128)(2,1)S(1)}, bf16[2,2,128,256]{3,2,0,1:T(8,128)(2,1)}) conditional(s32[]{:T(128)} %convert_element_type.543, (bf16[2,2,128,256]{2,3,0,1:T(8,128)(2,1)S(1)}) %tuple.340, (bf16[2,2,128,256]{2,3,0,1:T(8,128)(2,1)S(1)}, pred[3]{0:T(512)(128)(4,1)S(1)}, bf16[2,3,128,256]{2,1,3,0:T(4,128)(2,1)S(1)}, ...), branch_computations={%region_0.1_spmd, %region_1.8_spmd} | conditional | flops 608305152 | bytes 22544540 | solution.py:144
  15.6 0.7 fusion.681
  16.8 2.0 %conditional = (bf16[2,2,128,256]{3,2,0,1:T(8,128)(2,1)S(1)}) conditional(s32[]{:T(128)} %bitcast.58, bf16[2,2,128,256]{3,2,0,1:T(8,128)(2,1)S(1)} %copy.125, (bf16[2,3,128,256]{2,3,0,1:T(8,128)(2,1)S(1)}, bf16[2,2,128,256]{3,2,0,1:T(8,128)(2,1)S(1)}, bf16[3,2,128,128]{3,2,1,0:T(8,128)(2,1)S(1)}, bf16[3,2,256,256]{3,2,1,0:T(8,128)(2,1)S(1)}) %tuple.251), branch_computations={%region_2.2_spmd, %region_3.3_spmd} | conditional | flops 202506240 | bytes 6553608 | solution.py:57
  18.1 0.2 fusion.5
  18.6 0.2 fusion.4
  19.5 3.6 %conditional.1 = (bf16[2,2,128,256]{3,2,0,1:T(8,128)(2,1)S(1)}) conditional(s32[]{:T(128)} %bitcast.60, bf16[2,2,128,256]{3,2,0,1:T(8,128)(2,1)S(1)} %get-tuple-element.1046, (bf16[2,3,128,256]{2,3,0,1:T(8,128)(2,1)S(1)}, bf16[2,2,128,256]{3,2,0,1:T(8,128)(2,1)S(1)}, bf16[3,2,128,128]{3,2,1,0:T(8,128)(2,1)S(1)}, ...), branch_computations={%region_4.4_spmd, %region_5.5_spmd} | conditional | flops 202506240 | bytes 6553608 | solution.py:57
  19.6 0.8 copy.20
  20.4 1.0 multiply_convert_fusion.1
  22.4 0.2 fusion.33
  22.9 0.2 fusion.32
  23.9 4.3 %conditional.2 = (bf16[2,2,128,256]{3,2,0,1:T(8,128)(2,1)}) conditional(s32[]{:T(128)} %bitcast.62, bf16[2,2,128,256]{3,2,0,1:T(8,128)(2,1)S(1)} %get-tuple-element.1047, (bf16[2,3,128,256]{2,3,0,1:T(8,128)(2,1)S(1)}, bf16[2,2,128,256]{3,2,0,1:T(8,128)(2,1)S(1)}, bf16[3,2,128,128]{3,2,1,0:T(8,128)(2,1)S(1)}, ...), branch_computations={%region_6.6_spmd, %region_7.7_spmd} | conditional | flops 202506240 | bytes 6553608 | solution.py:57
  23.9 0.8 copy.21
  24.8 1.0 multiply_convert_fusion.2
  27.5 0.7 pad_maximum_fusion.2
  28.3 1.1 copy.127
  29.4 1.3 collective-permute-start.2
  30.7 3.3 %collective-permute-done.2 = bf16[2,2,128,256]{2,3,0,1:T(8,128)(2,1)S(1)} collective-permute-done((bf16[2,2,128,256]{2,3,0,1:T(8,128)(2,1)S(1)}, bf16[2,2,128,256]{2,3,0,1:T(8,128)(2,1)S(1)}, u32[]{:S(2)}, u32[]{:S(2)}) %collective-permute-start.2) | collective-permute-done | bytes 262176 | tf_op jit(solution)/shard_map/ppermute | solution.py:23
  34.0 0.7 broadcast_select_fusion.2
  34.7 10.6 %collective-permute-start.3 = (bf16[2,2,128,256]{2,3,0,1:T(8,128)(2,1)}, bf16[2,2,128,256]{2,3,0,1:T(8,128)(2,1)S(1)}, u32[]{:S(2)}, u32[]{:S(2)}) collective-permute-start(bf16[2,2,128,256]{2,3,0,1:T(8,128)(2,1)} %get-tuple-element.957), channel_id=1, source_target_pairs={{0,64},{64,128},{128,192},{1,65},{65,129},{129,193},{2,66},{66,130... | collective-permute-start | bytes 786440 | tf_op jit(solution)/shard_map/ppermute | solution.py:23
  45.3 3.6 %collective-permute-done.3 = bf16[2,2,128,256]{2,3,0,1:T(8,128)(2,1)S(1)} collective-permute-done((bf16[2,2,128,256]{2,3,0,1:T(8,128)(2,1)}, bf16[2,2,128,256]{2,3,0,1:T(8,128)(2,1)S(1)}, u32[]{:S(2)}, u32[]{:S(2)}) %collective-permute-start.3) | collective-permute-done | bytes 262176 | tf_op jit(solution)/shard_map/ppermute | solution.py:23
  49.0 0.9 conditional.33
  49.0 0.9 copy.134
  49.8 3.7 %collective-permute-start.4 = (bf16[2,2,128,256]{3,2,0,1:T(8,128)(2,1)}, bf16[2,2,128,256]{3,2,0,1:T(8,128)(2,1)S(1)}, u32[]{:S(2)}, u32[]{:S(2)}) collective-permute-start(bf16[2,2,128,256]{3,2,0,1:T(8,128)(2,1)} %get-tuple-element.801), channel_id=1, source_target_pairs={{0,64},{64,128},{128,192},{1,65},{65,129},{129,193},{2,66},{66,130... | collective-permute-start | bytes 786440 | tf_op jit(solution)/shard_map/ppermute | solution.py:23
  53.6 4.6 %collective-permute-done.4 = bf16[2,2,128,256]{3,2,0,1:T(8,128)(2,1)S(1)} collective-permute-done((bf16[2,2,128,256]{3,2,0,1:T(8,128)(2,1)}, bf16[2,2,128,256]{3,2,0,1:T(8,128)(2,1)S(1)}, u32[]{:S(2)}, u32[]{:S(2)}) %collective-permute-start.4) | collective-permute-done | bytes 262176 | tf_op jit(solution)/shard_map/ppermute | solution.py:23
  58.2 1.1 conditional.35
  58.3 1.0 broadcast_in_dim.42
  59.5 1.3 collective-permute-start.5
  60.8 16.8 %collective-permute-done.5 = bf16[2,2,128,256]{2,3,0,1:T(8,128)(2,1)S(1)} collective-permute-done((bf16[2,2,128,256]{2,3,0,1:T(8,128)(2,1)S(1)}, bf16[2,2,128,256]{2,3,0,1:T(8,128)(2,1)S(1)}, u32[]{:S(2)}, u32[]{:S(2)}) %collective-permute-start.5) | collective-permute-done | bytes 262176 | tf_op jit(solution)/shard_map/ppermute | solution.py:23
  77.7 1.3 collective-permute-start.6
  79.0 8.9 %collective-permute-done.6 = bf16[2,2,128,256]{2,3,0,1:T(8,128)(2,1)S(1)} collective-permute-done((bf16[2,2,128,256]{2,3,0,1:T(8,128)(2,1)S(1)}, bf16[2,2,128,256]{2,3,0,1:T(8,128)(2,1)S(1)}, u32[]{:S(2)}, u32[]{:S(2)}) %collective-permute-start.6) | collective-permute-done | bytes 262176 | tf_op jit(solution)/shard_map/ppermute | solution.py:23
  88.0 1.3 collective-permute-start.7
  89.3 0.6 fusion.690
  93.9 42.9 %collective-permute-done.7 = bf16[2,2,128,256]{2,3,0,1:T(8,128)(2,1)S(1)} collective-permute-done((bf16[2,2,128,256]{2,3,0,1:T(8,128)(2,1)S(1)}, bf16[2,2,128,256]{2,3,0,1:T(8,128)(2,1)S(1)}, u32[]{:S(2)}, u32[]{:S(2)}) %collective-permute-start.7) | collective-permute-done | bytes 262176 | tf_op jit(solution)/shard_map/ppermute | solution.py:23
  136.8 14.9 %conditional.38 = (f32[2,3,128,256]{3,2,0,1:T(8,128)}) conditional(s32[]{:T(128)} %convert_element_type.536, f32[2,3,128,256]{3,2,0,1:T(8,128)} %get-tuple-element.806, (pred[3]{0:T(512)(128)(4,1)S(1)}, bf16[2,3,2,128,256]{4,3,0,2,1:T(8,128)(2,1)S(1)}, pred[]{:T(512)}, bf16[2,2,128,256]{2,3,0,1:T(8,128)(2,1)S(1)}, ...), branch_computations={%region_54.55_spmd, %region_55.62_spmd} | conditional | flops 609419264 | bytes 32243952 | solution.py:168
  136.8 0.7 copy-done.18
  137.5 0.8 slice_bitcast_fusion.125
  138.2 0.3 copy.148
  138.5 1.0 broadcast_select_fusion
  139.5 0.7 fusion.688
  140.9 2.2 %conditional.20 = (bf16[2,2,128,256]{3,2,0,1:T(8,128)(2,1)S(1)}) conditional(s32[]{:T(128)} %convert_element_type.520, (bf16[2,2,128,256]{2,3,0,1:T(8,128)(2,1)S(1)}) %tuple.339, (bf16[2,3,128,256]{3,2,0,1:T(8,128)(2,1)S(1)}, bf16[2,2,128,256]{3,2,0,1:T(8,128)(2,1)}, bf16[2,2,128,256]{2,3,0,1:T(8,128)(2,1)S(1)}, ...), branch_computations={%region_56.56_spmd, %region_57.57_spmd} | conditional | flops 202440704 | bytes 7340068 | solution.py:89
  142.5 0.2 fusion.585
  143.8 1.9 %conditional.21 = (bf16[2,2,128,256]{3,2,0,1:T(8,128)(2,1)S(1)}) conditional(s32[]{:T(128)} %convert_element_type.519, bf16[2,2,128,256]{3,2,0,1:T(8,128)(2,1)S(1)} %get-tuple-element.1066, (bf16[2,3,128,256]{3,2,0,1:T(8,128)(2,1)S(1)}, bf16[2,2,128,256]{3,2,0,1:T(8,128)(2,1)S(1)}, bf16[2,2,128,256]{3,2,0,1:T(8,128)(2,1)S(1)}, ...), branch_computations={%region_58.58_spmd, %region_59.59_spmd} | conditional | flops 202440704 | bytes 6815752 | solution.py:89
  145.4 0.2 fusion.619
  146.4 1.9 %conditional.22 = (bf16[2,2,128,256]{3,2,0,1:T(8,128)(2,1)S(1)}) conditional(s32[]{:T(128)} %convert_element_type.518, bf16[2,2,128,256]{3,2,0,1:T(8,128)(2,1)S(1)} %get-tuple-element.1067, (bf16[2,3,128,256]{3,2,0,1:T(8,128)(2,1)S(1)}, bf16[2,2,128,256]{3,2,0,1:T(8,128)(2,1)S(1)}, bf16[2,2,128,256]{3,2,0,1:T(8,128)(2,1)S(1)}, ...), branch_computations={%region_60.60_spmd, %region_61.61_spmd} | conditional | flops 202440704 | bytes 6815752 | solution.py:89
  148.0 0.2 fusion.646
  148.5 1.4 fusion.673
  150.0 0.7 fusion.675
  150.7 1.0 pad_maximum_fusion.18
  151.7 1.0 slice_bitcast_fusion.127
  152.8 5.5 %dynamic_update_slice.8 = f32[3,128,768]{2,1,0:T(8,128)S(1)} dynamic-update-slice(f32[3,128,768]{2,1,0:T(8,128)S(1)} %broadcast_in_dim.58, f32[3,128,256]{2,1,0:T(8,128)S(1)} %slice_bitcast_fusion.127, s32[]{:T(128)} %constant.49.clone.1, s32[]{:T(128)} %constant.49.clone.1, s32[]{:T(128)S(6)} %select_n.192) | dynamic-update-slice | bytes 786436 | tf_op jit(solution)/shard_map/dynamic_update_slice | solution.py:103
  158.3 1.2 fusion.678
  159.5 5.5 %dynamic_update_slice.10 = f32[3,128,768]{2,1,0:T(8,128)S(1)} dynamic-update-slice(f32[3,128,768]{2,1,0:T(8,128)S(1)} %dynamic_update_slice.8, f32[3,128,256]{2,1,0:T(8,128)S(1)} %fusion.678, s32[]{:T(128)} %constant.49.clone.1, s32[]{:T(128)} %constant.49.clone.1, s32[]{:T(128)S(6)} %select_n.193) | dynamic-update-slice | bytes 786436 | tf_op jit(solution)/shard_map/dynamic_update_slice | solution.py:103
  165.0 10.4 %collective-permute-start.8 = (bf16[3,128,256]{2,1,0:T(8,128)(2,1)S(1)}, bf16[3,128,256]{2,1,0:T(8,128)(2,1)S(1)}, u32[]{:S(2)}, u32[]{:S(2)}) collective-permute-start(bf16[3,128,256]{2,1,0:T(8,128)(2,1)S(1)} %get-tuple-element.1018), channel_id=1, source_target_pairs={{0,1},{1,2},{2,3},{3,4},{4,5},{5,6},{6,7},{7,8},{8,9},{9,10},{10,1... | collective-permute-start | bytes 589832 | tf_op jit(solution)/shard_map/ppermute | solution.py:14
  175.5 1.9 %collective-permute-start.9 = (bf16[3,128,256]{2,1,0:T(8,128)(2,1)S(1)}, bf16[3,128,256]{2,1,0:T(8,128)(2,1)S(1)}, u32[]{:S(2)}, u32[]{:S(2)}) collective-permute-start(bf16[3,128,256]{2,1,0:T(8,128)(2,1)S(1)} %get-tuple-element.1019), channel_id=1, source_target_pairs={{1,0},{2,1},{3,2},{4,3},{5,4},{6,5},{7,6},{8,7},{9,8},{10,9},{11,1... | collective-permute-start | bytes 589832 | tf_op jit(solution)/shard_map/ppermute | solution.py:15
  177.4 0.7 collective-permute-done.8
  178.1 4.4 %collective-permute-done.9 = bf16[3,128,256]{2,1,0:T(8,128)(2,1)S(1)} collective-permute-done((bf16[3,128,256]{2,1,0:T(8,128)(2,1)S(1)}, bf16[3,128,256]{2,1,0:T(8,128)(2,1)S(1)}, u32[]{:S(2)}, u32[]{:S(2)}) %collective-permute-start.9) | collective-permute-done | bytes 196640 | tf_op jit(solution)/shard_map/ppermute | solution.py:15
  182.5 0.8 fusion.677
  (88 shorter events, 10.4 us)
Async XLA Ops:
  0.0 9.8 %copy-start.19 = (s32[2]{0:T(128)S(1)}, s32[2]{0:T(128)}, u32[]{:S(2)}) copy-start(s32[2]{0:T(128)} %param.69) | copy-start | bytes 28
  1.1 8.8 %collective-permute-start = (bf16[3,128,256]{1,0,2:T(4,128)(2,1)S(1)}, bf16[3,128,256]{1,0,2:T(4,128)(2,1)S(1)}, u32[]{:S(2)}, u32[]{:S(2)}) collective-permute-start(bf16[3,128,256]{1,0,2:T(4,128)(2,1)S(1)} %bitcast.1299), channel_id=1, source_target_pairs={{0,1},{1,2},{2,3},{3,4},{4,5},{5,6},{6,7},{7,8},{8,9},{9,10},{10,1... | collective-permute-start | bytes 589832 | tf_op jit(solution)/shard_map/ppermute | solution.py:14
  6.1 7.7 %collective-permute-start.1 = (bf16[3,128,256]{1,0,2:T(4,128)(2,1)S(1)}, bf16[3,128,256]{1,0,2:T(4,128)(2,1)S(1)}, u32[]{:S(2)}, u32[]{:S(2)}) collective-permute-start(bf16[3,128,256]{1,0,2:T(4,128)(2,1)S(1)} %bitcast.1300), channel_id=1, source_target_pairs={{1,0},{2,1},{3,2},{4,3},{5,4},{6,5},{7,6},{8,7},{9,8},{10,9},{11,1... | collective-permute-start | bytes 589832 | tf_op jit(solution)/shard_map/ppermute | solution.py:15
  9.9 5.5 %copy-start = (bf16[1,3,2,256,256]{4,3,2,1,0:T(8,128)(2,1)S(1)}, bf16[1,3,2,256,256]{4,3,2,1,0:T(8,128)(2,1)}, u32[]{:S(2)}) copy-start(bf16[1,3,2,256,256]{4,3,2,1,0:T(8,128)(2,1)} %param.73) | copy-start | bytes 2359300
  9.9 5.5 %copy-start.1 = (bf16[1,3,2,128,128]{4,3,2,1,0:T(8,128)(2,1)S(1)}, bf16[1,3,2,128,128]{4,3,2,1,0:T(8,128)(2,1)}, u32[]{:S(2)}) copy-start(bf16[1,3,2,128,128]{4,3,2,1,0:T(8,128)(2,1)} %param.72) | copy-start | bytes 589828
  29.4 4.6 %collective-permute-start.2 = (bf16[2,2,128,256]{2,3,0,1:T(8,128)(2,1)S(1)}, bf16[2,2,128,256]{2,3,0,1:T(8,128)(2,1)S(1)}, u32[]{:S(2)}, u32[]{:S(2)}) collective-permute-start(bf16[2,2,128,256]{2,3,0,1:T(8,128)(2,1)S(1)} %copy.127), channel_id=1, source_target_pairs={{0,64},{64,128},{128,192},{1,65},{65,129},{129,193},{2,66},{66,130... | collective-permute-start | bytes 786440 | tf_op jit(solution)/shard_map/ppermute | solution.py:23
  34.7 14.2 %collective-permute-start.3 = (bf16[2,2,128,256]{2,3,0,1:T(8,128)(2,1)}, bf16[2,2,128,256]{2,3,0,1:T(8,128)(2,1)S(1)}, u32[]{:S(2)}, u32[]{:S(2)}) collective-permute-start(bf16[2,2,128,256]{2,3,0,1:T(8,128)(2,1)} %get-tuple-element.957), channel_id=1, source_target_pairs={{0,64},{64,128},{128,192},{1,65},{65,129},{129,193},{2,66},{66,130... | collective-permute-start | bytes 786440 | tf_op jit(solution)/shard_map/ppermute | solution.py:23
  48.9 9.2 %copy-start.16 = (bf16[2,2,128,256]{3,2,1,0:T(8,128)(2,1)S(1)}, bf16[2,2,128,256]{3,2,1,0:T(8,128)(2,1)}, u32[]{:S(2)}) copy-start(bf16[2,2,128,256]{3,2,1,0:T(8,128)(2,1)} %param.68) | copy-start | bytes 786436
  49.8 8.3 %collective-permute-start.4 = (bf16[2,2,128,256]{3,2,0,1:T(8,128)(2,1)}, bf16[2,2,128,256]{3,2,0,1:T(8,128)(2,1)S(1)}, u32[]{:S(2)}, u32[]{:S(2)}) collective-permute-start(bf16[2,2,128,256]{3,2,0,1:T(8,128)(2,1)} %get-tuple-element.801), channel_id=1, source_target_pairs={{0,64},{64,128},{128,192},{1,65},{65,129},{129,193},{2,66},{66,130... | collective-permute-start | bytes 786440 | tf_op jit(solution)/shard_map/ppermute | solution.py:23
  59.5 18.1 %collective-permute-start.5 = (bf16[2,2,128,256]{2,3,0,1:T(8,128)(2,1)S(1)}, bf16[2,2,128,256]{2,3,0,1:T(8,128)(2,1)S(1)}, u32[]{:S(2)}, u32[]{:S(2)}) collective-permute-start(bf16[2,2,128,256]{2,3,0,1:T(8,128)(2,1)S(1)} %copy.141), channel_id=1, source_target_pairs={{64,0},{128,64},{192,128},{65,1},{129,65},{193,129},{66,2},{130,66... | collective-permute-start | bytes 786440 | tf_op jit(solution)/shard_map/ppermute | solution.py:23
  77.7 10.2 %collective-permute-start.6 = (bf16[2,2,128,256]{2,3,0,1:T(8,128)(2,1)S(1)}, bf16[2,2,128,256]{2,3,0,1:T(8,128)(2,1)S(1)}, u32[]{:S(2)}, u32[]{:S(2)}) collective-permute-start(bf16[2,2,128,256]{2,3,0,1:T(8,128)(2,1)S(1)} %get-tuple-element.959), channel_id=1, source_target_pairs={{64,0},{128,64},{192,128},{65,1},{129,65},{193,129},{66,2},{130,66... | collective-permute-start | bytes 786440 | tf_op jit(solution)/shard_map/ppermute | solution.py:23
  88.0 48.8 %collective-permute-start.7 = (bf16[2,2,128,256]{2,3,0,1:T(8,128)(2,1)S(1)}, bf16[2,2,128,256]{2,3,0,1:T(8,128)(2,1)S(1)}, u32[]{:S(2)}, u32[]{:S(2)}) collective-permute-start(bf16[2,2,128,256]{2,3,0,1:T(8,128)(2,1)S(1)} %get-tuple-element.960), channel_id=1, source_target_pairs={{64,0},{128,64},{192,128},{65,1},{129,65},{193,129},{66,2},{130,66... | collective-permute-start | bytes 786440 | tf_op jit(solution)/shard_map/ppermute | solution.py:23
  136.8 0.7 copy-start.18
  142.1 1.0 copy-start.13
  165.0 13.0 %collective-permute-start.8 = (bf16[3,128,256]{2,1,0:T(8,128)(2,1)S(1)}, bf16[3,128,256]{2,1,0:T(8,128)(2,1)S(1)}, u32[]{:S(2)}, u32[]{:S(2)}) collective-permute-start(bf16[3,128,256]{2,1,0:T(8,128)(2,1)S(1)} %get-tuple-element.1018), channel_id=1, source_target_pairs={{0,1},{1,2},{2,3},{3,4},{4,5},{5,6},{6,7},{7,8},{8,9},{9,10},{10,1... | collective-permute-start | bytes 589832 | tf_op jit(solution)/shard_map/ppermute | solution.py:14
  175.5 7.0 %collective-permute-start.9 = (bf16[3,128,256]{2,1,0:T(8,128)(2,1)S(1)}, bf16[3,128,256]{2,1,0:T(8,128)(2,1)S(1)}, u32[]{:S(2)}, u32[]{:S(2)}) collective-permute-start(bf16[3,128,256]{2,1,0:T(8,128)(2,1)S(1)} %get-tuple-element.1019), channel_id=1, source_target_pairs={{1,0},{2,1},{3,2},{4,3},{5,4},{6,5},{7,6},{8,7},{9,8},{10,9},{11,1... | collective-permute-start | bytes 589832 | tf_op jit(solution)/shard_map/ppermute | solution.py:15
where the time goes:
time: 184 us; the launch traced here: 183 us
  waiting for transfers between devices  89 us (48%)
  starting transfers between devices  38.6 us (21%)
  local copies, waits for them, and re-layouts  24.9 us (14%)
  other arithmetic  11 us (6%)
  matrix products  9.7 us (5%)
  between operations  5.04 us (3%)
  loops' own time  4.9 us (3%)
    ppermute x6, waiting for transfers between devices, shifted(): return lax.ppermute(array, axis, pairs)  80.1 us
    ppermute x6, starting transfers between devices, shifted(): return lax.ppermute(array, axis, pairs)  19.4 us
    ppermute x2, starting transfers between devices, padded(): before = lax.ppermute(last, axis, up)  15.4 us
    dynamic_update_slice x2, local copies, waits for them, and re-layouts, place_shots(): lax.dynamic_update_slice_in_dim(canvas, placed, offsets[shot_index], 2)  10.9 us
    ppermute x2, waiting for transfers between devices, padded(): after = lax.ppermute(leading, axis, down)  8.25 us
    ppermute x2, starting transfers between devices, padded(): after = lax.ppermute(leading, axis, down)  3.84 us
  transfers between devices with their start and end apart: 10, of which 9 were waited for; matrix products, arithmetic and copies ran while one was open for 1% of the time, Pallas kernels for 0%

commit v1 on v0

v1 whole, which is shorter than its diff:
```python
import functools

import jax
import jax.numpy as jnp
from jax import lax
from jax.experimental import pallas as pl
from jax.experimental.pallas import tpu as pltpu
from jax.sharding import PartitionSpec as P

MESH = pl.DeviceIdType.MESH
F32 = jnp.float32
BF16 = jnp.bfloat16


def dot_nn(a, b):
    return lax.dot_general(a, b, (((1,), (0,)), ((), ())), preferred_element_type=F32)


def dot_nt(a, b):
    return lax.dot_general(a, b, (((1,), (1,)), ((), ())), preferred_element_type=F32)


def kernel(
    nx, nt,
    source, anchors, counts, reflect, lx, ly, out,
    refl_own, refl_left, lxv, yv, xb, xbt, sel_own, sel_left, win,
    down_in, down_out, up_in, up_out, stored, corr, img_out, img_in,
    local_sem, refl_send, refl_recv, down_send, down_recv, up_send, up_recv, img_send, img_recv,
):
    slots, rows, width = refl_own.shape
    shots = down_in.shape[0]
    x = lax.axis_index("depth")
    t = lax.axis_index("tile")

    def remote(src, dst, send, recv, target):
        return pltpu.make_async_remote_copy(
            src_ref=src, dst_ref=dst, send_sem=send, recv_sem=recv,
            device_id=target, device_id_type=MESH,
        )

    to_below = (jnp.minimum(x + 1, nx - 1), t)
    to_above = (jnp.maximum(x - 1, 0), t)
    to_right = (x, jnp.minimum(t + 1, nt - 1))
    to_left = (x, jnp.maximum(t - 1, 0))

    copies = [
        pltpu.make_async_copy(lx.at[0], lxv, local_sem.at[0]),
        pltpu.make_async_copy(reflect.at[0], refl_own, local_sem.at[1]),
        pltpu.make_async_copy(ly.at[0], yv, local_sem.at[2]),
    ]
    for copy in copies:
        copy.start()

    barrier = pltpu.get_barrier_semaphore()
    neighbours = (
        (lax.rem(x + 1, nx), t), (lax.rem(x + nx - 1, nx), t),
        (x, lax.rem(t + 1, nt)), (x, lax.rem(t + nt - 1, nt)),
    )
    for neighbour in neighbours:
        pl.semaphore_signal(barrier, inc=1, device_id=neighbour, device_id_type=MESH)

    refl_copies = [
        remote(reflect.at[0, l], refl_left.at[l], refl_send.at[l], refl_recv.at[l], to_right)
        for l in range(slots)
    ]
    down_copies = [
        remote(down_out.at[k], down_in.at[k], down_send.at[k], down_recv.at[k], to_below)
        for k in range(shots)
    ]
    up_copies = [
        remote(up_out.at[k], up_in.at[k], up_send.at[k], up_recv.at[k], to_above)
        for k in range(shots)
    ]
    img_copies = [
        remote(img_out.at[l], img_in.at[l], img_send.at[l], img_recv.at[l], to_left)
        for l in range(slots)
    ]
    source_copies = [
        pltpu.make_async_copy(source.at[k], down_in.at[k], local_sem.at[3 + k])
        for k in range(shots)
    ]

    @pl.when(x == 0)
    def _():
        for copy in source_copies:
            copy.start()

    pl.semaphore_wait(barrier, 4)

    @pl.when(t < nt - 1)
    def _():
        for copy in refl_copies:
            copy.start()

    level_count = counts[0]
    i_r = lax.broadcasted_iota(jnp.int32, (rows, rows), 0)
    i_c = lax.broadcasted_iota(jnp.int32, (rows, rows), 1)
    eye_x = (i_r == i_c).astype(F32)
    j_r = lax.broadcasted_iota(jnp.int32, (width, width), 0)
    j_c = lax.broadcasted_iota(jnp.int32, (width, width), 1)
    live = [(level_count > l).astype(F32) for l in range(slots)]
    copies[0].wait()
    for l in range(slots):
        x_re = lxv[l, 0].astype(F32)
        x_im = lxv[l, 1].astype(F32)
        if l > 0:
            x_re = x_re * live[l] + eye_x * (1.0 - live[l])
            x_im = x_im * live[l]
        xb[l, :rows, :rows] = x_re.astype(BF16)
        xb[l, :rows, rows:] = (-x_im).astype(BF16)
        xb[l, rows:, :rows] = x_im.astype(BF16)
        xb[l, rows:, rows:] = x_re.astype(BF16)
        x_ret = x_re.T
        x_imt = x_im.T
        xbt[l, :rows, :rows] = x_ret.astype(BF16)
        xbt[l, :rows, rows:] = (-x_imt).astype(BF16)
        xbt[l, rows:, :rows] = x_imt.astype(BF16)
        xbt[l, rows:, rows:] = x_ret.astype(BF16)
    copies[2].wait()
    eye_y = (j_r == j_c).astype(F32)
    for l in range(1, slots):
        yv[l, 0] = (yv[l, 0].astype(F32) * live[l] + eye_y * (1.0 - live[l])).astype(BF16)
        yv[l, 1] = (yv[l, 1].astype(F32) * live[l]).astype(BF16)

    for k in range(shots):
        offset = anchors[k] - (t - 1) * width
        sel_left[:, k * width : (k + 1) * width] = (j_r - j_c == offset).astype(BF16)
        sel_own[:, k * width : (k + 1) * width] = (j_r - j_c == offset - width).astype(BF16)
    copies[1].wait()
    for l in range(slots):
        win[l] = dot_nn(refl_own[l], sel_own[...]) * live[l]

    @pl.when(t == 0)
    def _():
        refl_left[...] = jnp.zeros_like(refl_left)

    for l in range(slots):
        @pl.when(t > 0)
        def _(l=l):
            refl_copies[l].wait_recv()
        win[l] += dot_nn(refl_left[l], sel_left[...]) * live[l]

    def window(k, l):
        return win[l, :, k * width : (k + 1) * width]

    def descend(k):
        @pl.when(x == 0)
        def _():
            source_copies[k].wait()

        @pl.when(x > 0)
        def _():
            down_copies[k].wait_recv()

        for l in range(slots):
            gain = 1.0 + window(k, l)
            entering = down_in.at[k] if l == 0 else stored.at[k, l - 1]
            scaled = jnp.concatenate(
                [
                    (gain * entering[:rows].astype(F32)).astype(BF16),
                    (gain * entering[rows:].astype(F32)).astype(BF16),
                ],
                axis=0,
            )
            middle = dot_nn(xb[l], scaled).astype(BF16)
            by_re = dot_nt(middle, yv[l, 0])
            by_im = dot_nt(middle, yv[l, 1])
            leaving = stored.at[k, l] if l < slots - 1 else down_out.at[k]
            leaving[:rows] = (by_re[:rows] - by_im[rows:]).astype(BF16)
            leaving[rows:] = (by_im[:rows] + by_re[rows:]).astype(BF16)

        @pl.when(x < nx - 1)
        def _():
            down_copies[k].start()

    def ascend(k, last):
        if last:
            up_in[k] = jnp.zeros_like(up_in[k])
        else:
            up_copies[k].wait_recv()
        upgoing = up_in[k]
        for l in reversed(range(slots)):
            back = dot_nn(xbt[l], upgoing).astype(BF16)
            by_re = dot_nn(back, yv[l, 0])
            by_im = dot_nn(back, yv[l, 1])
            downward = down_in.at[k] if l == 0 else stored.at[k, l - 1]
            gain = window(k, l)
            d_re = downward[:rows].astype(F32)
            d_im = downward[rows:].astype(F32)
            u_re = (gain * d_re + (by_re[:rows] - by_im[rows:])).astype(BF16)
            u_im = (gain * d_im + (by_im[:rows] + by_re[rows:])).astype(BF16)
            if l > 0:
                upgoing = jnp.concatenate([u_re, u_im], axis=0)
            else:
                up_out[k, :rows] = u_re
                up_out[k, rows:] = u_im
            product = (d_re * u_re.astype(F32) + d_im * u_im.astype(F32)) * live[l]
            corr[l, :, k * width : (k + 1) * width] = product.astype(BF16)

        @pl.when(x > 0)
        def _():
            up_copies[k].start()

    @pl.when(x < nx - 1)
    def _():
        for k in range(shots):
            descend(k)
        for k in range(shots):
            ascend(k, False)

    @pl.when(x == nx - 1)
    def _():
        for k in range(shots):
            descend(k)
            ascend(k, True)

    for l in reversed(range(slots)):
        img_out[l] = dot_nt(corr[l], sel_left[...]).astype(BF16)

        @pl.when(t > 0)
        def _(l=l):
            img_copies[l].start()

    for l in reversed(range(slots)):
        out[0, l] = dot_nt(corr[l], sel_own[...])

    @pl.when(t < nt - 1)
    def _():
        for l in reversed(range(slots)):
            img_copies[l].wait_recv()
            out[0, l] += img_in[l].astype(F32)

    @pl.when(t < nt - 1)
    def _():
        for copy in refl_copies:
            copy.wait_send()

    @pl.when(x < nx - 1)
    def _():
        for copy in down_copies:
            copy.wait_send()

    @pl.when(x > 0)
    def _():
        for copy in up_copies:
            copy.wait_send()

    @pl.when(t > 0)
    def _():
        for copy in img_copies:
            copy.wait_send()


def solution(mesh):
    nx, nt = mesh.shape["depth"], mesh.shape["tile"]

    def on_device(source, anchors, counts, reflect, lateral_x, lateral_y):
        shots, _, rows, width = source.shape
        slots = reflect.shape[1]
        any_spec = pl.BlockSpec(memory_space=pl.ANY)
        smem = pl.BlockSpec(memory_space=pltpu.SMEM)
        wave = (shots, 2 * rows, width)
        dma = pltpu.SemaphoreType.DMA
        return pl.pallas_call(
            functools.partial(kernel, nx, nt),
            out_shape=jax.ShapeDtypeStruct((1, slots, rows, width), F32),
            in_specs=[any_spec, smem, smem, any_spec, any_spec, any_spec],
            out_specs=pl.BlockSpec(memory_space=pltpu.VMEM),
            scratch_shapes=[
                pltpu.VMEM((slots, rows, width), BF16),
                pltpu.VMEM((slots, rows, width), BF16),
                pltpu.VMEM((slots, 2, rows, rows), BF16),
                pltpu.VMEM((slots, 2, width, width), BF16),
                pltpu.VMEM((slots, 2 * rows, 2 * rows), BF16),
                pltpu.VMEM((slots, 2 * rows, 2 * rows), BF16),
                pltpu.VMEM((width, shots * width), BF16),
                pltpu.VMEM((width, shots * width), BF16),
                pltpu.VMEM((slots, rows, shots * width), F32),
                pltpu.VMEM(wave, BF16),
                pltpu.VMEM(wave, BF16),
                pltpu.VMEM(wave, BF16),
                pltpu.VMEM(wave, BF16),
                pltpu.VMEM((shots, slots - 1, 2 * rows, width), BF16),
                pltpu.VMEM((slots, rows, shots * width), BF16),
                pltpu.VMEM((slots, rows, width), BF16),
                pltpu.VMEM((slots, rows, width), BF16),
                dma((3 + shots,)),
                dma((slots,)), dma((slots,)),
                dma((shots,)), dma((shots,)),
                dma((shots,)), dma((shots,)),
                dma((slots,)), dma((slots,)),
            ],
            compiler_params=pltpu.CompilerParams(collective_id=0, has_side_effects=True),
        )(source.reshape(wave), anchors, counts, reflect, lateral_x, lateral_y)

    return jax.shard_map(
        on_device,
        mesh=mesh,
        in_specs=(
            P("tile", None, None, None),
            P("tile"),
            P("depth"),
            P("depth", None, None, "tile"),
            P("depth", None, None, None, None),
            P("depth", None, None, None, None),
        ),
        out_specs=P("depth", None, None, "tile"),
        check_vma=False,
    )
```

time: 184 us -> 55.1 us (0.30)
  the two profiles are of different devices: /device:TPU:1 before, /device:TPU:24 now
where the time goes in v1:
time: 55.1 us; the launch traced here: 55 us
  Pallas kernels  52.6 us (95%)
  local copies, waits for them, and re-layouts  1.77 us (3%)
  between operations  0.66 us (1%)
    pallas_call x1, Pallas kernels, on_device(): pl.pallas_call(functools.partial(kernel, nx, nt), out_shape=jax.ShapeDtyp...  52.6 us
    unnamed x1, local copies, waits for them, and re-layouts  1.77 us

profile of v1, /device:TPU:24, one launch (start us, length us, event | category | flops | bytes accessed | tf_op | source)
XLA Modules:
  0.0 55.0 jit_solution(9327729068187521376)
XLA Ops:
  0.7 52.6 %shard_map.64 = f32[1,3,128,256]{3,2,1,0:T(8,128)} custom-call(bf16[2,256,256]{2,1,0:T(8,128)(2,1)} %bitcast.1, s32[2]{0:T(128)} %anchors.1, s32[1]{0:T(128)S(6)} %copy.8.counts, bf16[1,3,128,256]{3,2,1,0:T(8,128)(2,1)} %reflect.1, bf16[1,3,2,128,128]{4,3,2,1,0:T(8,128)(2,1)} %lx.1, bf16[1,3,2,256,256]{4,3,2,1,0:T(8,128)(2,1)} %ly.1), custom_call_target="tpu_custom_call" | custom-call | tf_op jit(solution)/shard_map/pallas_call | solution.py:264
  53.2 1.8 %copy.9 = f32[1,3,128,256]{3,2,1,0:T(8,128)} copy(f32[1,3,128,256]{3,2,1,0:T(8,128)} %shard_map.64) | data formatting | bytes 786432

commit v2 on v1

v2 whole, which is shorter than its diff:
```python
import functools

import jax
import jax.numpy as jnp
from jax import lax
from jax.experimental import pallas as pl
from jax.experimental.pallas import tpu as pltpu
from jax.sharding import PartitionSpec as P

MESH = pl.DeviceIdType.MESH
F32 = jnp.float32
BF16 = jnp.bfloat16


def dot_nn(a, b):
    return lax.dot_general(a, b, (((1,), (0,)), ((), ())), preferred_element_type=F32)


def dot_nt(a, b):
    return lax.dot_general(a, b, (((1,), (1,)), ((), ())), preferred_element_type=F32)


def complex_dot(a_re, a_im, b_re, b_im):
    re = dot_nn(a_re, b_re) - dot_nn(a_im, b_im)
    im = dot_nn(a_re, b_im) + dot_nn(a_im, b_re)
    return re.astype(BF16), im.astype(BF16)


def kernel(
    nt,
    source, anchors_hbm, counts_hbm, reflect, lx, ly, out,
    anchors, counts, refl_own, refl_left, lxv, yv, xb, xbt, sel_own, sel_left, win,
    waves, late, early, early_out, own_x, own_y, comp_x, comp_y, comp_out_x, comp_out_y,
    corr, img_out, img_in,
    local_sem, refl_send, refl_recv, down_send, down_recv, late_send, late_recv,
    early_send, early_recv, comp_send, comp_recv, img_send, img_recv,
):
    slots, rows, width = refl_own.shape
    shots = waves.shape[0]
    x = lax.axis_index("depth")
    t = lax.axis_index("tile")

    def remote(src, dst, send, recv, target):
        return pltpu.make_async_remote_copy(
            src_ref=src, dst_ref=dst, send_sem=send, recv_sem=recv,
            device_id=target, device_id_type=MESH,
        )

    copies = [
        pltpu.make_async_copy(lx.at[0], lxv, local_sem.at[0]),
        pltpu.make_async_copy(reflect.at[0], refl_own, local_sem.at[1]),
        pltpu.make_async_copy(ly.at[0], yv, local_sem.at[2]),
        pltpu.make_async_copy(anchors_hbm, anchors, local_sem.at[3]),
        pltpu.make_async_copy(counts_hbm, counts, local_sem.at[4]),
    ]
    for copy in copies:
        copy.start()

    barrier = pltpu.get_barrier_semaphore()
    neighbours = (
        (lax.rem(x + 1, 4), t), (lax.rem(x + 2, 4), t), (lax.rem(x + 3, 4), t),
        (x, lax.rem(t + 1, nt)), (x, lax.rem(t + nt - 1, nt)),
    )
    for neighbour in neighbours:
        pl.semaphore_signal(barrier, inc=1, device_id=neighbour, device_id_type=MESH)

    to_below = (jnp.minimum(x + 1, 3), t)
    to_above = (jnp.maximum(x - 1, 0), t)
    to_right = (x, jnp.minimum(t + 1, nt - 1))
    to_left = (x, jnp.maximum(t - 1, 0))

    def refl_copy(l):
        return remote(reflect.at[0, l], refl_left.at[l], refl_send.at[l], refl_recv.at[l], to_right)

    def img_copy(l):
        return remote(img_out.at[l], img_in.at[l], img_send.at[l], img_recv.at[l], to_left)

    def down_copy(k):
        return remote(
            waves.at[k, slots], waves.at[k, 0], down_send.at[k], down_recv.at[k], to_below
        )

    def late_copy(k, target):
        sem = late_send.at[k, target]
        return remote(late.at[k], late_in.at[k], sem, late_recv.at[k], (target, t))

    def early_copy(k):
        return remote(early_out.at[k], early.at[k], early_send.at[k], early_recv.at[k], to_above)

    def comp_copies():
        return [
            remote(comp_out_x, comp_x, comp_send.at[0], comp_recv.at[0], to_above),
            remote(comp_out_y, comp_y, comp_send.at[1], comp_recv.at[1], to_above),
        ]

    late_in = late
    source_copies = [
        pltpu.make_async_copy(source.at[k], waves.at[k, 0], local_sem.at[5 + k])
        for k in range(shots)
    ]

    @pl.when(x == 0)
    def _():
        for copy in source_copies:
            copy.start()

    pl.semaphore_wait(barrier, 5)

    @pl.when(t < nt - 1)
    def _():
        for l in range(slots):
            refl_copy(l).start()

    j_r = lax.broadcasted_iota(jnp.int32, (width, width), 0)
    j_c = lax.broadcasted_iota(jnp.int32, (width, width), 1)
    copies[3].wait()
    for k in range(shots):
        offset = anchors[k] - (t - 1) * width
        sel_left[k] = (j_r - j_c == offset).astype(BF16)
        sel_own[k] = (j_r - j_c == offset - width).astype(BF16)
    copies[4].wait()
    level_count = counts[0]

    def live(l):
        return (level_count > l).astype(F32)

    i_r = lax.broadcasted_iota(jnp.int32, (rows, rows), 0)
    i_c = lax.broadcasted_iota(jnp.int32, (rows, rows), 1)
    eye_x = (i_r == i_c).astype(F32)
    copies[0].wait()
    for l in range(slots):
        x_re = lxv[l, 0].astype(F32)
        x_im = lxv[l, 1].astype(F32)
        if l > 0:
            x_re = x_re * live(l) + eye_x * (1.0 - live(l))
            x_im = x_im * live(l)
        xb[l, :rows, :rows] = x_re.astype(BF16)
        xb[l, :rows, rows:] = (-x_im).astype(BF16)
        xb[l, rows:, :rows] = x_im.astype(BF16)
        xb[l, rows:, rows:] = x_re.astype(BF16)
        x_ret = x_re.T
        x_imt = x_im.T
        xbt[l, :rows, :rows] = x_ret.astype(BF16)
        xbt[l, :rows, rows:] = (-x_imt).astype(BF16)
        xbt[l, rows:, :rows] = x_imt.astype(BF16)
        xbt[l, rows:, rows:] = x_ret.astype(BF16)
    copies[2].wait()
    eye_y = (j_r == j_c).astype(F32)
    for l in range(1, slots):
        yv[l, 0] = (yv[l, 0].astype(F32) * live(l) + eye_y * (1.0 - live(l))).astype(BF16)
        yv[l, 1] = (yv[l, 1].astype(F32) * live(l)).astype(BF16)
    copies[1].wait()
    for l in range(slots):
        for k in range(shots):
            win[k, l] = dot_nn(refl_own[l], sel_own[k]) * live(l)

    def finish_window(l):
        @pl.when(t > 0)
        def _():
            refl_copy(l).wait_recv()
            for k in range(shots):
                win[k, l] += dot_nn(refl_left[l], sel_left[k]) * live(l)

    def descend(k, with_windows=False):
        def level(l):
            if with_windows:
                finish_window(l)
            gain = 1.0 + win[k, l]
            scaled = jnp.concatenate(
                [
                    (gain * waves[k, l, :rows].astype(F32)).astype(BF16),
                    (gain * waves[k, l, rows:].astype(F32)).astype(BF16),
                ],
                axis=0,
            )
            middle = dot_nn(xb[l], scaled).astype(BF16)
            by_re = dot_nt(middle, yv[l, 0])
            by_im = dot_nt(middle, yv[l, 1])
            waves[k, l + 1, :rows] = (by_re[:rows] - by_im[rows:]).astype(BF16)
            waves[k, l + 1, rows:] = (by_im[:rows] + by_re[rows:]).astype(BF16)

        each_level(level)

    def each_level(level, backwards=False):
        for i in range(slots):
            level(slots - 1 - i if backwards else i)

    def ascend(wave, k, images):
        def level(l):
            back = dot_nn(xbt[l], wave[k]).astype(BF16)
            by_re = dot_nn(back, yv[l, 0])
            by_im = dot_nn(back, yv[l, 1])
            gain = win[k, l]
            d_re = waves[k, l, :rows].astype(F32)
            d_im = waves[k, l, rows:].astype(F32)
            u_re = (gain * d_re + (by_re[:rows] - by_im[rows:])).astype(BF16)
            u_im = (gain * d_im + (by_im[:rows] + by_re[rows:])).astype(BF16)
            wave[k, :rows] = u_re
            wave[k, rows:] = u_im
            if images:
                product = (d_re * u_re.astype(F32) + d_im * u_im.astype(F32)) * live(l)
                corr[k, l] = product.astype(BF16)
                if k == shots - 1:
                    finish_image(l)

        each_level(level, True)

    def finish_image(l):
        left = dot_nt(corr[0, l], sel_left[0])
        for k in range(1, shots):
            left += dot_nt(corr[k, l], sel_left[k])
        img_out[l] = left.astype(BF16)

        @pl.when(t > 0)
        def _():
            img_copy(l).start()

        own = dot_nt(corr[0, l], sel_own[0])
        for k in range(1, shots):
            own += dot_nt(corr[k, l], sel_own[k])
        out[0, l] = own

    def compose():
        own_x[...] = dot_nn(xbt[slots - 2], xbt[slots - 1]).astype(BF16)
        own_y[0], own_y[1] = yv[slots - 1, 0], yv[slots - 1, 1]
        for l in reversed(range(slots - 1)):
            if l < slots - 2:
                own_x[...] = dot_nn(xbt[l], own_x[...]).astype(BF16)
            own_y[0], own_y[1] = complex_dot(own_y[0], own_y[1], yv[l, 0], yv[l, 1])

    def carry_over(k):
        back = dot_nn(comp_x[...], late[k]).astype(BF16)
        by_re = dot_nn(back, comp_y[0])
        by_im = dot_nn(back, comp_y[1])
        held_re = early[k, :rows].astype(F32)
        held_im = early[k, rows:].astype(F32)
        late[k, :rows] = (held_re + (by_re[:rows] - by_im[rows:])).astype(BF16)
        late[k, rows:] = (held_im + (by_im[:rows] + by_re[rows:])).astype(BF16)

    @pl.when(x == 0)
    def _():
        for k in range(shots):
            source_copies[k].wait()
            descend(k, k == 0)
            down_copy(k).start()
        for copy in comp_copies():
            copy.wait_recv()
        for k in range(shots):
            early_copy(k).wait_recv()
            late_copy(k, 0).wait_recv()
            carry_over(k)
            ascend(late, k, True)

    @pl.when(x > 0)
    def _():
        for l in range(slots):
            finish_window(l)

    @pl.when(x == 1)
    def _():
        compose()
        for k in range(shots):
            down_copy(k).wait_recv()
            descend(k)
            down_copy(k).start()
        for copy in comp_copies():
            copy.wait_recv()
        comp_out_x[...] = dot_nn(own_x[...], comp_x[...]).astype(BF16)
        comp_out_y[0], comp_out_y[1] = complex_dot(comp_y[0], comp_y[1], own_y[0], own_y[1])
        for copy in comp_copies():
            copy.start()
        for k in range(shots):
            early_copy(k).wait_recv()
            early_out[k] = early[k]
            ascend(early_out, k, False)
            early_copy(k).start()
        for k in range(shots):
            late_copy(k, 1).wait_recv()
            carry_over(k)
            ascend(late, k, True)

    @pl.when(x == 2)
    def _():
        compose()
        comp_out_x[...] = own_x[...]
        comp_out_y[...] = own_y[...]
        for copy in comp_copies():
            copy.start()
        for k in range(shots):
            down_copy(k).wait_recv()
            descend(k)
            down_copy(k).start()
            early_out[k] = jnp.zeros_like(early_out[k])
            ascend(early_out, k, False)
            early_copy(k).start()
        for k in range(shots):
            late_copy(k, 2).wait_recv()
            ascend(late, k, True)

    @pl.when(x == 3)
    def _():
        for k in range(shots):
            down_copy(k).wait_recv()
            descend(k)
            late[k] = jnp.zeros_like(late[k])
            ascend(late, k, True)
            for target in (1, 0, 2):
                late_copy(k, target).start()

    @pl.when(t < nt - 1)
    def _():
        for l in reversed(range(slots)):
            img_copy(l).wait_recv()
            out[0, l] += img_in[l].astype(F32)
        for l in range(slots):
            refl_copy(l).wait_send()

    @pl.when(x < 3)
    def _():
        for k in range(shots):
            down_copy(k).wait_send()

    @pl.when((x == 1) | (x == 2))
    def _():
        for k in range(shots):
            early_copy(k).wait_send()
        for copy in comp_copies():
            copy.wait_send()

    @pl.when(x == 3)
    def _():
        for k in range(shots):
            for target in range(3):
                late_copy(k, target).wait_send()

    @pl.when(t > 0)
    def _():
        for l in range(slots):
            img_copy(l).wait_send()


def solution(mesh):
    nt = mesh.shape["tile"]

    def on_device(source, anchors, counts, reflect, lateral_x, lateral_y):
        shots, _, rows, width = source.shape
        slots = reflect.shape[1]
        any_spec = pl.BlockSpec(memory_space=pltpu.HBM)
        wave = (shots, 2 * rows, width)
        dma = pltpu.SemaphoreType.DMA
        return pl.pallas_call(
            functools.partial(kernel, nt),
            out_shape=jax.ShapeDtypeStruct((1, slots, rows, width), F32),
            in_specs=[any_spec] * 6,
            out_specs=pl.BlockSpec(memory_space=pltpu.VMEM),
            scratch_shapes=[
                pltpu.SMEM((shots,), jnp.int32),
                pltpu.SMEM((1,), jnp.int32),
                pltpu.VMEM((slots, rows, width), BF16),
                pltpu.VMEM((slots, rows, width), BF16),
                pltpu.VMEM((slots, 2, rows, rows), BF16),
                pltpu.VMEM((slots, 2, width, width), BF16),
                pltpu.VMEM((slots, 2 * rows, 2 * rows), BF16),
                pltpu.VMEM((slots, 2 * rows, 2 * rows), BF16),
                pltpu.VMEM((shots, width, width), BF16),
                pltpu.VMEM((shots, width, width), BF16),
                pltpu.VMEM((shots, slots, rows, width), F32),
                pltpu.VMEM((shots, slots + 1, 2 * rows, width), BF16),
                pltpu.VMEM(wave, BF16),
                pltpu.VMEM(wave, BF16),
                pltpu.VMEM(wave, BF16),
                pltpu.VMEM((2 * rows, 2 * rows), BF16),
                pltpu.VMEM((2, width, width), BF16),
                pltpu.VMEM((2 * rows, 2 * rows), BF16),
                pltpu.VMEM((2, width, width), BF16),
                pltpu.VMEM((2 * rows, 2 * rows), BF16),
                pltpu.VMEM((2, width, width), BF16),
                pltpu.VMEM((shots, slots, rows, width), BF16),
                pltpu.VMEM((slots, rows, width), BF16),
                pltpu.VMEM((slots, rows, width), BF16),
                dma((5 + shots,)),
                dma((slots,)), dma((slots,)),
                dma((shots,)), dma((shots,)),
                dma((shots, 3)), dma((shots,)),
                dma((shots,)), dma((shots,)),
                dma((2,)), dma((2,)),
                dma((slots,)), dma((slots,)),
            ],
            compiler_params=pltpu.CompilerParams(
                collective_id=0, has_side_effects=True, vmem_limit_bytes=64_000_000
            ),
        )(source.reshape(wave), anchors, counts, reflect, lateral_x, lateral_y)

    return jax.shard_map(
        on_device,
        mesh=mesh,
        in_specs=(
            P("tile", None, None, None),
            P("tile"),
            P("depth"),
            P("depth", None, None, "tile"),
            P("depth", None, None, None, None),
            P("depth", None, None, None, None),
        ),
        out_specs=P("depth", None, None, "tile"),
        check_vma=False,
    )
```

time: 55.1 us -> 46.8 us (0.85)
  the two profiles are of different devices: /device:TPU:24 before, /device:TPU:5 now
where the time goes in v2:
time: 46.8 us; the launch traced here: 46.7 us
  Pallas kernels  44.3 us (95%)
  local copies, waits for them, and re-layouts  1.77 us (4%)
  between operations  0.66 us (1%)
    pallas_call x1, Pallas kernels, on_device(): pl.pallas_call(functools.partial(kernel, nt), out_shape=jax.ShapeDtypeStr...  44.3 us
    unnamed x1, local copies, waits for them, and re-layouts  1.77 us

profile of v2, /device:TPU:5, one launch (start us, length us, event | category | flops | bytes accessed | tf_op | source)
XLA Modules:
  0.0 46.7 jit_solution(4702351590351554854)
XLA Ops:
  0.7 44.3 %shard_map.64 = f32[1,3,128,256]{3,2,1,0:T(8,128)} custom-call(bf16[2,256,256]{2,1,0:T(8,128)(2,1)} %bitcast.1, s32[2]{0:T(128)} %anchors_hbm.1, s32[1]{0:T(128)S(6)} %copy.8.counts_hbm, bf16[1,3,128,256]{3,2,1,0:T(8,128)(2,1)} %reflect.1, bf16[1,3,2,128,128]{4,3,2,1,0:T(8,128)(2,1)} %lx.1, bf16[1,3,2,256,256]{4,3,2,1,0:T(8,128)(2,1)} %ly.1), custom_call_target="tpu_custom_call" | custom-call | tf_op jit(solution)/shard_map/pallas_call | solution.py:351
  44.9 1.8 %copy.9 = f32[1,3,128,256]{3,2,1,0:T(8,128)} copy(f32[1,3,128,256]{3,2,1,0:T(8,128)} %shard_map.64) | data formatting | bytes 786432

commit v3 on v2

--- a/solution.py
+++ b/solution.py
@@ -18,6 +18,10 @@
 
 def dot_nt(a, b):
     return lax.dot_general(a, b, (((1,), (1,)), ((), ())), preferred_element_type=F32)
+
+
+def in_hbm(array):
+    return pltpu.with_memory_space_constraint(array, pltpu.HBM)
 
 
 def complex_dot(a_re, a_im, b_re, b_im):
@@ -200,7 +204,7 @@
             if images:
                 product = (d_re * u_re.astype(F32) + d_im * u_im.astype(F32)) * live(l)
                 corr[k, l] = product.astype(BF16)
-                if k == shots - 1:
+                if images == "place" and k == shots - 1:
                     finish_image(l)
 
         each_level(level, True)
@@ -249,7 +253,7 @@
             early_copy(k).wait_recv()
             late_copy(k, 0).wait_recv()
             carry_over(k)
-            ascend(late, k, True)
+            ascend(late, k, "place")
 
     @pl.when(x > 0)
     def _():
@@ -277,7 +281,7 @@
         for k in range(shots):
             late_copy(k, 1).wait_recv()
             carry_over(k)
-            ascend(late, k, True)
+            ascend(late, k, "place")
 
     @pl.when(x == 2)
     def _():
@@ -295,7 +299,7 @@
             early_copy(k).start()
         for k in range(shots):
             late_copy(k, 2).wait_recv()
-            ascend(late, k, True)
+            ascend(late, k, "place")
 
     @pl.when(x == 3)
     def _():
@@ -306,6 +310,8 @@
             ascend(late, k, True)
             for target in (1, 0, 2):
                 late_copy(k, target).start()
+        for l in range(slots):
+            finish_image(l)
 
     @pl.when(t < nt - 1)
     def _():
@@ -387,9 +393,9 @@
                 dma((slots,)), dma((slots,)),
             ],
             compiler_params=pltpu.CompilerParams(
-                collective_id=0, has_side_effects=True, vmem_limit_bytes=64_000_000
+                collective_id=0, has_side_effects=True, vmem_limit_bytes=16 * 1024 * 1024
             ),
-        )(source.reshape(wave), anchors, counts, reflect, lateral_x, lateral_y)
+        )(in_hbm(source.reshape(wave)), in_hbm(anchors), counts, in_hbm(reflect), in_hbm(lateral_x), in_hbm(lateral_y))
 
     return jax.shard_map(
         on_device,

time: 46.8 us -> 45.1 us (0.964)
  local copies, waits for them, and re-layouts: 1.77 us -> 0.75 us
  Pallas kernels: 44.3 us -> 43.5 us
    unnamed x1, local copies, waits for them, and re-layouts: 1.77 us -> 0.75 us
    pallas_call x1, Pallas kernels: 44.3 us -> 43.5 us  [on_device(): pl.pallas_call(functools.partial(kernel, nt), out_shape=jax.ShapeDtypeStr...]
where the time goes in v3:
time: 45.1 us; the launch traced here: 45 us
  Pallas kernels  43.5 us (96%)
  local copies, waits for them, and re-layouts  0.75 us (2%)
  between operations  0.66 us (1%)
    pallas_call x1, Pallas kernels, on_device(): pl.pallas_call(functools.partial(kernel, nt), out_shape=jax.ShapeDtypeStr...  43.5 us

profile of v3, /device:TPU:5, one launch (start us, length us, event | category | flops | bytes accessed | tf_op | source)
XLA Modules:
  0.0 45.0 jit_solution(4845248143752534685)
XLA Ops:
  0.7 43.5 %shard_map.64 = f32[1,3,128,256]{3,2,1,0:T(8,128)S(1)} custom-call(bf16[2,256,256]{2,1,0:T(8,128)(2,1)} %bitcast.1, s32[2]{0:T(128)} %anchors_hbm.1, s32[1]{0:T(128)S(6)} %copy.8.counts_hbm, bf16[1,3,128,256]{3,2,1,0:T(8,128)(2,1)} %reflect.1, bf16[1,3,2,128,128]{4,3,2,1,0:T(8,128)(2,1)} %lx.1, bf16[1,3,2,256,256]{4,3,2,1,0:T(8,128)(2,1)} %ly.1), custom_call_target="tpu_custom_call" | custom-call | tf_op jit(solution)/shard_map/pallas_call | solution.py:357
  44.2 0.7 %copy.9 = f32[1,3,128,256]{3,2,1,0:T(8,128)} copy(f32[1,3,128,256]{3,2,1,0:T(8,128)S(1)} %shard_map.64) | data formatting | bytes 786432

commit v4 on v3

--- a/solution.py
+++ b/solution.py
@@ -34,10 +34,11 @@
     nt,
     source, anchors_hbm, counts_hbm, reflect, lx, ly, out,
     anchors, counts, refl_own, refl_left, lxv, yv, xb, xbt, sel_own, sel_left, win,
-    waves, late, early, early_out, own_x, own_y, comp_x, comp_y, comp_out_x, comp_out_y,
-    corr, img_out, img_in,
+    waves, late, early, early_out, own_x, own_y, comp_x, comp_y, both_x, both_y,
+    near_x, near_y, kept, left_acc, corr, img_out, img_in,
     local_sem, refl_send, refl_recv, down_send, down_recv, late_send, late_recv,
-    early_send, early_recv, comp_send, comp_recv, img_send, img_recv,
+    early_send, early_recv, comp_send, comp_recv, near_send, near_recv,
+    img_send, img_recv,
 ):
     slots, rows, width = refl_own.shape
     shots = waves.shape[0]
@@ -57,13 +58,13 @@
         pltpu.make_async_copy(anchors_hbm, anchors, local_sem.at[3]),
         pltpu.make_async_copy(counts_hbm, counts, local_sem.at[4]),
     ]
-    for copy in copies:
-        copy.start()
+    for i in (1, 3, 4, 0, 2):
+        copies[i].start()
 
     barrier = pltpu.get_barrier_semaphore()
     neighbours = (
-        (lax.rem(x + 1, 4), t), (lax.rem(x + 2, 4), t), (lax.rem(x + 3, 4), t),
-        (x, lax.rem(t + 1, nt)), (x, lax.rem(t + nt - 1, nt)),
+        (lax.rem(x + 2, 4), t), (x, lax.rem(t + 1, nt)), (x, lax.rem(t + nt - 1, nt)),
+        (lax.rem(x + 1, 4), t), (lax.rem(x + 3, 4), t),
     )
     for neighbour in neighbours:
         pl.semaphore_signal(barrier, inc=1, device_id=neighbour, device_id_type=MESH)
@@ -74,7 +75,7 @@
     to_left = (x, jnp.maximum(t - 1, 0))
 
     def refl_copy(l):
-        return remote(reflect.at[0, l], refl_left.at[l], refl_send.at[l], refl_recv.at[l], to_right)
+        return remote(refl_own.at[l], refl_left.at[l], refl_send.at[l], refl_recv.at[l], to_right)
 
     def img_copy(l):
         return remote(img_out.at[l], img_in.at[l], img_send.at[l], img_recv.at[l], to_left)
@@ -91,10 +92,16 @@
     def early_copy(k):
         return remote(early_out.at[k], early.at[k], early_send.at[k], early_recv.at[k], to_above)
 
-    def comp_copies():
+    def comp_copies(target):
         return [
-            remote(comp_out_x, comp_x, comp_send.at[0], comp_recv.at[0], to_above),
-            remote(comp_out_y, comp_y, comp_send.at[1], comp_recv.at[1], to_above),
+            remote(own_x, comp_x, comp_send.at[0, target], comp_recv.at[0], (target, t)),
+            remote(own_y, comp_y, comp_send.at[1, target], comp_recv.at[1], (target, t)),
+        ]
+
+    def near_copies():
+        return [
+            remote(own_x, near_x, near_send.at[0], near_recv.at[0], to_above),
+            remote(own_y, near_y, near_send.at[1], near_recv.at[1], to_above),
         ]
 
     late_in = late
@@ -108,6 +115,7 @@
         for copy in source_copies:
             copy.start()
 
+    copies[1].wait()
     pl.semaphore_wait(barrier, 5)
 
     @pl.when(t < nt - 1)
@@ -153,22 +161,24 @@
     for l in range(1, slots):
         yv[l, 0] = (yv[l, 0].astype(F32) * live(l) + eye_y * (1.0 - live(l))).astype(BF16)
         yv[l, 1] = (yv[l, 1].astype(F32) * live(l)).astype(BF16)
-    copies[1].wait()
     for l in range(slots):
         for k in range(shots):
             win[k, l] = dot_nn(refl_own[l], sel_own[k]) * live(l)
 
-    def finish_window(l):
+    def finish_window(l, first_shot=True, others=True):
         @pl.when(t > 0)
         def _():
-            refl_copy(l).wait_recv()
-            for k in range(shots):
-                win[k, l] += dot_nn(refl_left[l], sel_left[k]) * live(l)
-
-    def descend(k, with_windows=False):
+            if first_shot:
+                refl_copy(l).wait_recv()
+                win[0, l] += dot_nn(refl_left[l], sel_left[0]) * live(l)
+            if others:
+                for k in range(1, shots):
+                    win[k, l] += dot_nn(refl_left[l], sel_left[k]) * live(l)
+
+    def descend(k, with_windows=False, steps=slots):
         def level(l):
             if with_windows:
-                finish_window(l)
+                finish_window(l, k == 0, k == 1)
             gain = 1.0 + win[k, l]
             scaled = jnp.concatenate(
                 [
@@ -183,46 +193,56 @@
             waves[k, l + 1, :rows] = (by_re[:rows] - by_im[rows:]).astype(BF16)
             waves[k, l + 1, rows:] = (by_im[:rows] + by_re[rows:]).astype(BF16)
 
-        each_level(level)
-
-    def each_level(level, backwards=False):
-        for i in range(slots):
-            level(slots - 1 - i if backwards else i)
-
-    def ascend(wave, k, images):
+        for l in range(steps):
+            level(l)
+
+    def ascend(wave, k, images=None, from_zero=False, last=False):
         def level(l):
-            back = dot_nn(xbt[l], wave[k]).astype(BF16)
-            by_re = dot_nn(back, yv[l, 0])
-            by_im = dot_nn(back, yv[l, 1])
             gain = win[k, l]
             d_re = waves[k, l, :rows].astype(F32)
             d_im = waves[k, l, rows:].astype(F32)
-            u_re = (gain * d_re + (by_re[:rows] - by_im[rows:])).astype(BF16)
-            u_im = (gain * d_im + (by_im[:rows] + by_re[rows:])).astype(BF16)
+            if from_zero and l == slots - 1:
+                u_re = (gain * d_re).astype(BF16)
+                u_im = (gain * d_im).astype(BF16)
+            else:
+                back = dot_nn(xbt[l], wave[k]).astype(BF16)
+                by_re = dot_nn(back, yv[l, 0])
+                by_im = dot_nn(back, yv[l, 1])
+                u_re = (gain * d_re + (by_re[:rows] - by_im[rows:])).astype(BF16)
+                u_im = (gain * d_im + (by_im[:rows] + by_re[rows:])).astype(BF16)
             wave[k, :rows] = u_re
             wave[k, rows:] = u_im
-            if images:
+            if images == "keep":
+                kept[k, l, :rows] = u_re
+                kept[k, l, rows:] = u_im
+            if images == "place":
                 product = (d_re * u_re.astype(F32) + d_im * u_im.astype(F32)) * live(l)
                 corr[k, l] = product.astype(BF16)
-                if images == "place" and k == shots - 1:
-                    finish_image(l)
-
-        each_level(level, True)
-
-    def finish_image(l):
-        left = dot_nt(corr[0, l], sel_left[0])
-        for k in range(1, shots):
-            left += dot_nt(corr[k, l], sel_left[k])
-        img_out[l] = left.astype(BF16)
+                if last:
+                    image_left(l, k)
+
+        for l in reversed(range(slots)):
+            level(l)
+        if images == "place":
+            for l in reversed(range(slots)):
+                if last:
+                    image_own(l, k)
+                else:
+                    image_first(l, k)
+
+    def image_first(l, k):
+        left_acc[l] = dot_nt(corr[k, l], sel_left[k])
+        out[0, l] = dot_nt(corr[k, l], sel_own[k])
+
+    def image_left(l, k):
+        img_out[l] = (left_acc[l] + dot_nt(corr[k, l], sel_left[k])).astype(BF16)
 
         @pl.when(t > 0)
         def _():
             img_copy(l).start()
 
-        own = dot_nt(corr[0, l], sel_own[0])
-        for k in range(1, shots):
-            own += dot_nt(corr[k, l], sel_own[k])
-        out[0, l] = own
+    def image_own(l, k):
+        out[0, l] += dot_nt(corr[k, l], sel_own[k])
 
     def compose():
         own_x[...] = dot_nn(xbt[slots - 2], xbt[slots - 1]).astype(BF16)
@@ -232,28 +252,30 @@
                 own_x[...] = dot_nn(xbt[l], own_x[...]).astype(BF16)
             own_y[0], own_y[1] = complex_dot(own_y[0], own_y[1], yv[l, 0], yv[l, 1])
 
-    def carry_over(k):
-        back = dot_nn(comp_x[...], late[k]).astype(BF16)
-        by_re = dot_nn(back, comp_y[0])
-        by_im = dot_nn(back, comp_y[1])
-        held_re = early[k, :rows].astype(F32)
-        held_im = early[k, rows:].astype(F32)
-        late[k, :rows] = (held_re + (by_re[:rows] - by_im[rows:])).astype(BF16)
-        late[k, rows:] = (held_im + (by_im[:rows] + by_re[rows:])).astype(BF16)
+    def carry_over(op_x, op_y, wave, held, k, into):
+        back = dot_nn(op_x[...], wave[k]).astype(BF16)
+        by_re = dot_nn(back, op_y[0])
+        by_im = dot_nn(back, op_y[1])
+        held_re = held[k, :rows].astype(F32)
+        held_im = held[k, rows:].astype(F32)
+        into[k, :rows] = (held_re + (by_re[:rows] - by_im[rows:])).astype(BF16)
+        into[k, rows:] = (held_im + (by_im[:rows] + by_re[rows:])).astype(BF16)
 
     @pl.when(x == 0)
     def _():
         for k in range(shots):
             source_copies[k].wait()
-            descend(k, k == 0)
+            descend(k, True)
             down_copy(k).start()
-        for copy in comp_copies():
+        for copy in near_copies() + comp_copies(0):
             copy.wait_recv()
+        both_x[...] = dot_nn(near_x[...], comp_x[...]).astype(BF16)
+        both_y[0], both_y[1] = complex_dot(comp_y[0], comp_y[1], near_y[0], near_y[1])
         for k in range(shots):
             early_copy(k).wait_recv()
             late_copy(k, 0).wait_recv()
-            carry_over(k)
-            ascend(late, k, "place")
+            carry_over(both_x, both_y, late, early, k, late)
+            ascend(late, k, "place", last=k == 1)
 
     @pl.when(x > 0)
     def _():
@@ -263,55 +285,60 @@
     @pl.when(x == 1)
     def _():
         compose()
+        for copy in near_copies():
+            copy.start()
         for k in range(shots):
             down_copy(k).wait_recv()
             descend(k)
             down_copy(k).start()
-        for copy in comp_copies():
+        for k in range(shots):
+            ascend(early_out, k, from_zero=True)
+        for k in range(shots):
+            early_copy(k).wait_recv()
+            carry_over(own_x, own_y, early, early_out, k, early_out)
+            early_copy(k).start()
+        for copy in comp_copies(1):
             copy.wait_recv()
-        comp_out_x[...] = dot_nn(own_x[...], comp_x[...]).astype(BF16)
-        comp_out_y[0], comp_out_y[1] = complex_dot(comp_y[0], comp_y[1], own_y[0], own_y[1])
-        for copy in comp_copies():
-            copy.start()
-        for k in range(shots):
-            early_copy(k).wait_recv()
-            early_out[k] = early[k]
-            ascend(early_out, k, False)
-            early_copy(k).start()
-        for k in range(shots):
+        for k in reversed(range(shots)):
             late_copy(k, 1).wait_recv()
-            carry_over(k)
-            ascend(late, k, "place")
+            carry_over(comp_x, comp_y, late, early, k, late)
+            ascend(late, k, "place", last=k == 0)
 
     @pl.when(x == 2)
     def _():
         compose()
-        comp_out_x[...] = own_x[...]
-        comp_out_y[...] = own_y[...]
-        for copy in comp_copies():
+        for copy in comp_copies(1) + comp_copies(0):
             copy.start()
         for k in range(shots):
             down_copy(k).wait_recv()
             descend(k)
             down_copy(k).start()
-            early_out[k] = jnp.zeros_like(early_out[k])
-            ascend(early_out, k, False)
+            ascend(early_out, k, from_zero=True)
             early_copy(k).start()
-        for k in range(shots):
-            late_copy(k, 2).wait_recv()
-            ascend(late, k, "place")
+        late_copy(0, 2).wait_recv()
+        late_copy(0, 1).start()
+        early[0] = late[0]
+        ascend(early, 0, "place")
+        late_copy(1, 2).wait_recv()
+        ascend(late, 1, "place", last=True)
 
     @pl.when(x == 3)
     def _():
         for k in range(shots):
             down_copy(k).wait_recv()
-            descend(k)
-            late[k] = jnp.zeros_like(late[k])
-            ascend(late, k, True)
-            for target in (1, 0, 2):
+            descend(k, steps=slots - 1)
+            ascend(late, k, "keep", from_zero=True)
+            for target in ((0, 2), (1, 0))[k]:
                 late_copy(k, target).start()
-        for l in range(slots):
-            finish_image(l)
+        late_copy(1, 1).wait_send()
+        late_copy(1, 2).start()
+        for l in reversed(range(slots)):
+            for k in range(shots):
+                product = waves[k, l].astype(F32) * kept[k, l].astype(F32)
+                corr[k, l] = ((product[:rows] + product[rows:]) * live(l)).astype(BF16)
+            image_first(l, 0)
+            image_left(l, 1)
+            image_own(l, 1)
 
     @pl.when(t < nt - 1)
     def _():
@@ -330,14 +357,24 @@
     def _():
         for k in range(shots):
             early_copy(k).wait_send()
-        for copy in comp_copies():
+    @pl.when(x == 1)
+    def _():
+        for copy in near_copies():
             copy.wait_send()
 
+    @pl.when(x == 2)
+    def _():
+        for copy in comp_copies(1) + comp_copies(0):
+            copy.wait_send()
+
     @pl.when(x == 3)
     def _():
-        for k in range(shots):
-            for target in range(3):
-                late_copy(k, target).wait_send()
+        for k, target in ((0, 0), (0, 2), (1, 0), (1, 2)):
+            late_copy(k, target).wait_send()
+
+    @pl.when(x == 2)
+    def _():
+        late_copy(0, 1).wait_send()
 
     @pl.when(t > 0)
     def _():
@@ -381,6 +418,10 @@
                 pltpu.VMEM((2, width, width), BF16),
                 pltpu.VMEM((2 * rows, 2 * rows), BF16),
                 pltpu.VMEM((2, width, width), BF16),
+                pltpu.VMEM((2 * rows, 2 * rows), BF16),
+                pltpu.VMEM((2, width, width), BF16),
+                pltpu.VMEM((shots, slots, 2 * rows, width), BF16),
+                pltpu.VMEM((slots, rows, width), F32),
                 pltpu.VMEM((shots, slots, rows, width), BF16),
                 pltpu.VMEM((slots, rows, width), BF16),
                 pltpu.VMEM((slots, rows, width), BF16),
@@ -389,6 +430,7 @@
                 dma((shots,)), dma((shots,)),
                 dma((shots, 3)), dma((shots,)),
                 dma((shots,)), dma((shots,)),
+                dma((2, 2)), dma((2,)),
                 dma((2,)), dma((2,)),
                 dma((slots,)), dma((slots,)),
             ],

time: 45.1 us -> 43.8 us (0.971); the launches traced: 45 us -> 43.1 us
  Pallas kernels: 43.5 us -> 41.7 us
    pallas_call x1, Pallas kernels: 43.5 us -> 41.7 us  [on_device(): pl.pallas_call(functools.partial(kernel, nt), out_shape=jax.ShapeDtypeStr...]
where the time goes in v4:
time: 43.8 us; the launch traced here: 43.1 us
  Pallas kernels  41.7 us (95%)
  local copies, waits for them, and re-layouts  0.75 us (2%)
  between operations  0.66 us (2%)
    pallas_call x1, Pallas kernels, on_device(): pl.pallas_call(functools.partial(kernel, nt), out_shape=jax.ShapeDtypeStr...  41.7 us

profile of v4, /device:TPU:5, one launch (start us, length us, event | category | flops | bytes accessed | tf_op | source)
XLA Modules:
  0.0 43.1 jit_solution(2263433849743857957)
XLA Ops:
  0.7 41.7 %shard_map.64 = f32[1,3,128,256]{3,2,1,0:T(8,128)S(1)} custom-call(bf16[2,256,256]{2,1,0:T(8,128)(2,1)} %bitcast.1, s32[2]{0:T(128)} %anchors_hbm.1, s32[1]{0:T(128)S(6)} %copy.8.counts_hbm, bf16[1,3,128,256]{3,2,1,0:T(8,128)(2,1)} %reflect.1, bf16[1,3,2,128,128]{4,3,2,1,0:T(8,128)(2,1)} %lx.1, bf16[1,3,2,256,256]{4,3,2,1,0:T(8,128)(2,1)} %ly.1), custom_call_target="tpu_custom_call" | custom-call | tf_op jit(solution)/shard_map/pallas_call | solution.py:394
  42.4 0.7 %copy.9 = f32[1,3,128,256]{3,2,1,0:T(8,128)} copy(f32[1,3,128,256]{3,2,1,0:T(8,128)S(1)} %shard_map.64) | data formatting | bytes 786432

commit v5 on v4

--- a/solution.py
+++ b/solution.py
@@ -150,12 +150,16 @@
         xb[l, :rows, rows:] = (-x_im).astype(BF16)
         xb[l, rows:, :rows] = x_im.astype(BF16)
         xb[l, rows:, rows:] = x_re.astype(BF16)
-        x_ret = x_re.T
-        x_imt = x_im.T
-        xbt[l, :rows, :rows] = x_ret.astype(BF16)
-        xbt[l, :rows, rows:] = (-x_imt).astype(BF16)
-        xbt[l, rows:, :rows] = x_imt.astype(BF16)
-        xbt[l, rows:, rows:] = x_ret.astype(BF16)
+
+    def transpose_operators():
+        for l in range(slots):
+            x_ret = xb[l, :rows, :rows].astype(F32).T
+            x_imt = xb[l, rows:, :rows].astype(F32).T
+            xbt[l, :rows, :rows] = x_ret.astype(BF16)
+            xbt[l, :rows, rows:] = (-x_imt).astype(BF16)
+            xbt[l, rows:, :rows] = x_imt.astype(BF16)
+            xbt[l, rows:, rows:] = x_ret.astype(BF16)
+
     copies[2].wait()
     eye_y = (j_r == j_c).astype(F32)
     for l in range(1, slots):
@@ -267,6 +271,7 @@
             source_copies[k].wait()
             descend(k, True)
             down_copy(k).start()
+        transpose_operators()
         for copy in near_copies() + comp_copies(0):
             copy.wait_recv()
         both_x[...] = dot_nn(near_x[...], comp_x[...]).astype(BF16)
@@ -279,6 +284,7 @@
 
     @pl.when(x > 0)
     def _():
+        transpose_operators()
         for l in range(slots):
             finish_window(l)
 

time: 43.8 us -> 43.8 us (level)
  no operation moved by 1% of the time
where the time goes in v5:
time: 43.8 us; the launch traced here: 43.1 us
  Pallas kernels  41.7 us (95%)
  local copies, waits for them, and re-layouts  0.75 us (2%)
  between operations  0.66 us (2%)
    pallas_call x1, Pallas kernels, on_device(): pl.pallas_call(functools.partial(kernel, nt), out_shape=jax.ShapeDtypeStr...  41.7 us

profile of v5, /device:TPU:5, one launch (start us, length us, event | category | flops | bytes accessed | tf_op | source)
XLA Modules:
  0.0 43.1 jit_solution(14067956189901512048)
XLA Ops:
  0.7 41.7 %shard_map.64 = f32[1,3,128,256]{3,2,1,0:T(8,128)S(1)} custom-call(bf16[2,256,256]{2,1,0:T(8,128)(2,1)} %bitcast.1, s32[2]{0:T(128)} %anchors_hbm.1, s32[1]{0:T(128)S(6)} %copy.8.counts_hbm, bf16[1,3,128,256]{3,2,1,0:T(8,128)(2,1)} %reflect.1, bf16[1,3,2,128,128]{4,3,2,1,0:T(8,128)(2,1)} %lx.1, bf16[1,3,2,256,256]{4,3,2,1,0:T(8,128)(2,1)} %ly.1), custom_call_target="tpu_custom_call" | custom-call | tf_op jit(solution)/shard_map/pallas_call | solution.py:400
  42.4 0.7 %copy.9 = f32[1,3,128,256]{3,2,1,0:T(8,128)} copy(f32[1,3,128,256]{3,2,1,0:T(8,128)S(1)} %shard_map.64) | data formatting | bytes 786432

commit v6 on v5

--- a/solution.py
+++ b/solution.py
@@ -279,8 +279,10 @@
         for k in range(shots):
             early_copy(k).wait_recv()
             late_copy(k, 0).wait_recv()
-            carry_over(both_x, both_y, late, early, k, late)
-            ascend(late, k, "place", last=k == 1)
+            if k == 0:
+                late_copy(0, 1).start()
+            carry_over(both_x, both_y, late, early, k, early)
+            ascend(early, k, "place", last=k == 1)
 
     @pl.when(x > 0)
     def _():
@@ -322,9 +324,7 @@
             ascend(early_out, k, from_zero=True)
             early_copy(k).start()
         late_copy(0, 2).wait_recv()
-        late_copy(0, 1).start()
-        early[0] = late[0]
-        ascend(early, 0, "place")
+        ascend(late, 0, "place")
         late_copy(1, 2).wait_recv()
         ascend(late, 1, "place", last=True)
 
@@ -334,10 +334,8 @@
             down_copy(k).wait_recv()
             descend(k, steps=slots - 1)
             ascend(late, k, "keep", from_zero=True)
-            for target in ((0, 2), (1, 0))[k]:
+            for target in ((0, 2), (1, 0, 2))[k]:
                 late_copy(k, target).start()
-        late_copy(1, 1).wait_send()
-        late_copy(1, 2).start()
         for l in reversed(range(slots)):
             for k in range(shots):
                 product = waves[k, l].astype(F32) * kept[k, l].astype(F32)
@@ -375,10 +373,10 @@
 
     @pl.when(x == 3)
     def _():
-        for k, target in ((0, 0), (0, 2), (1, 0), (1, 2)):
+        for k, target in ((0, 0), (0, 2), (1, 0), (1, 1), (1, 2)):
             late_copy(k, target).wait_send()
 
-    @pl.when(x == 2)
+    @pl.when(x == 0)
     def _():
         late_copy(0, 1).wait_send()
 

time: 43.8 us -> 43.8 us (level)
  the two profiles are of different devices: /device:TPU:5 before, /device:TPU:3 now
where the time goes in v6:
time: 43.8 us; the launch traced here: 43.7 us
  Pallas kernels  42.3 us (97%)
  local copies, waits for them, and re-layouts  0.75 us (2%)
  between operations  0.66 us (2%)
    pallas_call x1, Pallas kernels, on_device(): pl.pallas_call(functools.partial(kernel, nt), out_shape=jax.ShapeDtypeStr...  42.3 us

profile of v6, /device:TPU:3, one launch (start us, length us, event | category | flops | bytes accessed | tf_op | source)
XLA Modules:
  0.0 43.7 jit_solution(5491267041090253571)
XLA Ops:
  0.7 42.3 %shard_map.64 = f32[1,3,128,256]{3,2,1,0:T(8,128)S(1)} custom-call(bf16[2,256,256]{2,1,0:T(8,128)(2,1)} %bitcast.1, s32[2]{0:T(128)} %anchors_hbm.1, s32[1]{0:T(128)S(6)} %copy.8.counts_hbm, bf16[1,3,128,256]{3,2,1,0:T(8,128)(2,1)} %reflect.1, bf16[1,3,2,128,128]{4,3,2,1,0:T(8,128)(2,1)} %lx.1, bf16[1,3,2,256,256]{4,3,2,1,0:T(8,128)(2,1)} %ly.1), custom_call_target="tpu_custom_call" | custom-call | tf_op jit(solution)/shard_map/pallas_call | solution.py:398
  43.0 0.7 %copy.9 = f32[1,3,128,256]{3,2,1,0:T(8,128)} copy(f32[1,3,128,256]{3,2,1,0:T(8,128)S(1)} %shard_map.64) | data formatting | bytes 786432
